TPU v7x, 256 devices: a whole 4x4x8 slice. The times are simulated.
256 devices in a mesh: stream: 2 (over z_hi), dp: 16 (over x, y), tensor: 8 (over z_lo, core).
Axes of the slice: x: 4, y: 4, z: 8 (z_hi: 2, z_lo: 4; z = z_hi * 4 + z_lo), core: 2. Of those that a mesh axis runs over, the one named last changes fastest.
Arguments:
- hidden: bfloat16 [2, 256, 8192], P('stream', 'tensor', 'dp'), may hold values from -3 to 3
- cached_rotated_keys: bfloat16 [2, 256, 8, 256, 128], P('stream', 'dp', 'tensor'), may hold values from -6 to 6
- cached_values: bfloat16 [2, 256, 8, 256, 128], P('stream', 'dp', 'tensor'), may hold values from -18 to 18
- cache_lengths: int32 [2, 256], P('stream', 'dp'), may hold values from 1 to 256, as said below
- recent_ids: int32 [256, 128], replicated, may hold values from 0 to 65535
- guidance: float32 [256], replicated, may hold values from 1 to 3
- w_query: bfloat16 [8192, 8192], P('dp', 'tensor'), may hold values from -0.0625 to 0.0625
- key_value_weight: bfloat16 [8192, 2, 1024], P('dp', None, 'tensor'), may hold values from -0.0625 to 0.0625
- w_output: bfloat16 [8192, 8192], P('tensor', 'dp'), may hold values from -0.0625 to 0.0625
- norm_gain: bfloat16 [8192], P('dp'), may hold values from 0.5 to 1.5
- w_head: bfloat16 [8192, 65536], P(None, ('dp', 'tensor')), may hold values from -0.16503906 to 0.16503906
Outputs:
- guided_logprobs: float32 [256, 65536], P('stream', ('dp', 'tensor'))
Inputs may be any that keep to these rules, and one draw needn't show every extreme that they name: `cache_lengths`: every prompt has 1 to 256 filled slots in each stream; some prompt has all 256; lengths differ widely from one group of 16 prompts to the next.
All inputs are finite; a program needn't handle non-finite values.
Results may differ from a plain program's by a relative error of at most 0.0025.
Values may be sent and summed in bfloat16 or wider, within the bound.
A program may use at most 64 MiB of HBM per device.

v0:
```python
import jax
import jax.numpy as jnp
from jax import lax
from jax.sharding import PartitionSpec as P

MODEL_WIDTH = 8192
HEAD_SIZE = 128
rope_theta = 500000.0
penalty_step = 1.5
norm_eps = 1e-05


def partner_2(value, axis, distance):
    mask = 2**distance
    pairs = [(source, source ^ mask) for source in range(lax.axis_size(axis))]
    return lax.ppermute(value, axis, pairs)


def rotate(values, positions):
    halfway = values.shape[-1] // 2
    frequency = rope_theta ** (-(jnp.arange(halfway, dtype=jnp.float32) * 2.0 / values.shape[-1]))
    angles = positions.astype(jnp.float32)[:, None, None] * frequency
    cosine_term = jnp.cos(angles)
    sine_term = jnp.sin(angles)
    first_half = values[..., :halfway]
    second_half = values[..., halfway:]
    return jnp.concatenate(
        [
            first_half * cosine_term - second_half * sine_term,
            second_half * cosine_term + first_half * sine_term,
        ],
        axis=-1,
    )


def repeat_counts(recent_ids, first_column, width):
    columns = first_column + jnp.arange(width, dtype=jnp.int32)
    return jnp.sum((recent_ids[:, :, None] == columns[None, None, :]).astype(jnp.float32), 1)


def body(
    hidden,
    cached_rotated_keys,
    cached_values,
    cache_lengths,
    recent_ids,
    guidance,
    w_query,
    key_value_weight,
    w_output,
    norm_gain,
    w_head,
):
    local_width = hidden.shape[2]
    query_cols = w_query.shape[1]
    kv_cols = key_value_weight.shape[2]
    local_prompts = cache_lengths.shape[1]
    lengths = cache_lengths[0]
    vocab_local = w_head.shape[1]
    all_rows = lax.all_gather(hidden[0], "tensor", axis=0, tiled=True)
    kv_flat = key_value_weight.reshape(local_width, 2 * kv_cols)
    projected = lax.psum_scatter(
        jnp.concatenate(
            [
                jnp.dot(all_rows, w_query, preferred_element_type=jnp.float32),
                jnp.dot(all_rows, kv_flat, preferred_element_type=jnp.float32),
            ],
            axis=1,
        ),
        "dp",
        scatter_dimension=0,
        tiled=True,
    )
    query_heads = query_cols // HEAD_SIZE
    kv_heads = kv_cols // HEAD_SIZE
    rotated_query = rotate(
        projected[:, :query_cols].reshape(local_prompts, query_heads, HEAD_SIZE), lengths
    ).astype(jnp.bfloat16)
    key_value_rows = projected[:, query_cols:].reshape(local_prompts, 2, kv_heads, HEAD_SIZE)
    fresh_key = rotate(key_value_rows[:, 0], lengths).astype(jnp.bfloat16)
    value_new = key_value_rows[:, 1].astype(jnp.bfloat16)
    grouped_queries = rotated_query.reshape(
        local_prompts, kv_heads, query_heads // kv_heads, HEAD_SIZE
    )
    attention_scale = HEAD_SIZE ** (-0.5)
    key_block = cached_rotated_keys[0]
    value_block = cached_values[0]
    scores = (
        jnp.einsum(
            "pkgd,pksd->pkgs", grouped_queries, key_block, preferred_element_type=jnp.float32
        )
        * attention_scale
    )
    self_score = (
        jnp.einsum("pkgd,pkd->pkg", grouped_queries, fresh_key, preferred_element_type=jnp.float32)
        * attention_scale
    )
    valid = jnp.arange(key_block.shape[2], dtype=jnp.int32)[None, :] < lengths[:, None]
    exps = jnp.where(valid[:, None, None, :], jnp.exp(scores), 0.0)
    own_exp = jnp.exp(self_score)
    denominator = jnp.sum(exps, -1) + own_exp
    weights = (exps / denominator[..., None]).astype(jnp.bfloat16)
    own_weight = (own_exp / denominator).astype(jnp.bfloat16)
    attended = jnp.einsum(
        "pkgs,pksd->pkgd", weights, value_block, preferred_element_type=jnp.float32
    )
    attended = (
        attended
        + own_weight.astype(jnp.float32)[..., None] * value_new.astype(jnp.float32)[:, :, None, :]
    )
    attended = attended.reshape(local_prompts, query_cols).astype(jnp.bfloat16)
    partial_out = jnp.dot(
        lax.all_gather(attended, "dp", axis=0, tiled=True),
        w_output,
        preferred_element_type=jnp.float32,
    )
    output_sum = lax.psum_scatter(partial_out, "tensor", scatter_dimension=0, tiled=True)
    residual = (hidden[0].astype(jnp.float32) + output_sum).astype(jnp.bfloat16)
    widened = residual.astype(jnp.float32)
    squares = lax.psum(jnp.sum(widened * widened, 1), "dp")
    inverse = lax.rsqrt(squares / MODEL_WIDTH + norm_eps)
    normed = (widened * inverse[:, None] * norm_gain.astype(jnp.float32)).astype(jnp.bfloat16)
    normed_all = lax.all_gather(normed, "tensor", axis=0, tiled=True)
    logits = jnp.dot(
        lax.all_gather(normed_all, "dp", axis=1, tiled=True),
        w_head,
        preferred_element_type=jnp.float32,
    )
    stream_side = lax.axis_index("stream")
    half_rows = logits.shape[0] // 2
    mine_start = stream_side * half_rows
    other_start = (1 - stream_side) * half_rows
    column_base = lax.axis_index(("dp", "tensor")) * vocab_local
    mine = lax.dynamic_slice_in_dim(logits, mine_start, half_rows, 0)
    sending = lax.dynamic_slice_in_dim(logits, other_start, half_rows, 0)
    partner = partner_2(sending, "stream", 0)
    conditional = jnp.where(stream_side == 0, mine, partner)
    unconditional = jnp.where(stream_side == 0, partner, mine)
    guide = lax.dynamic_slice_in_dim(guidance, mine_start, half_rows, 0)[:, None]
    recent_mine = lax.dynamic_slice_in_dim(recent_ids, mine_start, half_rows, 0)
    guided = unconditional + guide * (conditional - unconditional)
    guided = guided - penalty_step * repeat_counts(recent_mine, column_base, vocab_local)
    totals = lax.psum(jnp.sum(jnp.exp(guided), 1), ("dp", "tensor"))
    return guided - jnp.log(totals)[:, None]


def solution(mesh):
    return jax.shard_map(
        body,
        mesh=mesh,
        in_specs=(
            P("stream", "tensor", "dp"),
            P("stream", "dp", "tensor", None, None),
            P("stream", "dp", "tensor", None, None),
            P("stream", "dp"),
            P(),
            P(),
            P("dp", "tensor"),
            P("dp", None, "tensor"),
            P("tensor", "dp"),
            P("dp"),
            P(None, ("dp", "tensor")),
        ),
        out_specs=P("stream", ("dp", "tensor")),
        check_vma=False,
    )
```

profile of v0, /device:TPU:128, one launch (start us, length us, event | category | flops | bytes accessed | tf_op | source)
XLA Modules:
  0.0 647.4 jit_solution(1154850240006349418)
XLA Ops:
  6.5 0.0 copy-start
  6.5 0.0 copy-start.6
  6.6 0.0 copy-start.4
  6.6 0.0 reduce-scatter.3.cloned.1.call-start
  6.6 14.5 %all-gather = bf16[1,256,512]{2,1,0:T(8,128)(2,1)S(1)} all-gather(bf16[1,32,512]{2,1,0:T(8,128)(2,1)} %param.11), channel_id=2, replica_groups=mesh['stream'=2,'dp'=16,'tensor'=8] {'tensor'}, dimensions={1}, use_global_device_ids=true | all-gather | bytes 294912 | tf_op jit(solution)/shard_map/all_gather | solution.py:60
  21.1 0.0 copy-done
  21.1 0.5 fusion.9
  21.6 1.2 fusion.5
  22.8 1.2 pad_maximum_fusion
  24.0 0.0 reduce-scatter.3.cloned.1.call-update
  24.0 0.0 reduce-scatter.5.cloned.1.call-start
  24.1 0.7 bitcast_convert_fusion
  24.7 0.7 iota_compare_fusion
  25.4 0.1 multiply_cosine_fusion.1
  25.6 79.2 %reduce-scatter.3.cloned.1.call-done = f32[16,1280]{1,0:T(8,128)} async-done(((f32[256,1280]{1,0:T(8,128)}), f32[16,1280]{1,0:T(8,128)}) %reduce-scatter.3.cloned.1.call-update) | async-done | bytes 81936 | tf_op jit(solution)/shard_map/reduce_scatter | solution.py:62
  104.8 0.7 slice.36
  105.6 0.1 fusion.30
  105.7 0.8 slice_bitcast_fusion
  106.6 0.1 maximum_bitcast_fusion
  106.6 0.1 subtract_convert_fusion
  106.7 0.2 fusion.25
  106.9 1.7 fusion.33
  108.7 0.0 copy-done.1
  108.7 0.3 fusion.2
  109.0 23.3 %all_gather.13 = bf16[256,1024]{1,0:T(8,128)(2,1)S(1)} all-gather(bf16[16,1024]{1,0:T(8,128)(2,1)S(1)} %bitcast.51), channel_id=1, replica_groups=mesh['stream'=2,'dp'=16,'tensor'=8] {'dp'}, dimensions={0}, use_global_device_ids=true | all-gather | bytes 557056 | tf_op jit(solution)/shard_map/all_gather | solution.py:113
  132.3 0.0 copy-done.2
  132.3 1.2 fusion.34
  133.5 0.0 reduce-scatter.5.cloned.1.call-update
  133.6 0.0 all-gather.3.cloned.1.call-start
  133.6 0.0 copy-done.5
  133.6 32.9 %reduce-scatter.5.cloned.1.call-done = f32[32,512]{1,0:T(8,128)} async-done(((f32[256,512]{1,0:T(8,128)}), f32[32,512]{1,0:T(8,128)}) %reduce-scatter.5.cloned.1.call-update) | async-done | bytes 65552 | tf_op jit(solution)/shard_map/reduce_scatter | solution.py:117
  166.5 0.0 copy-done.3
  166.5 1.0 fusion.11
  167.5 40.3 %psum.14 = f32[32]{0:T(128)S(1)} all-reduce(f32[32]{0:T(128)S(1)} %fusion.11), channel_id=1, replica_groups=mesh['stream'=2,'dp'=16,'tensor'=8] {'dp'}, use_global_device_ids=true, to_apply=%region_4.5 | all-reduce | flops 32 | bytes 256 | tf_op jit(solution)/shard_map/psum | solution.py:120
  207.8 0.9 fusion.13
  208.7 15.3 %all_gather.14 = bf16[256,512]{1,0:T(8,128)(2,1)} all-gather(bf16[32,512]{1,0:T(8,128)(2,1)S(1)} %fusion.13), channel_id=1, replica_groups=mesh['stream'=2,'dp'=16,'tensor'=8] {'tensor'}, dimensions={0}, use_global_device_ids=true | all-gather | bytes 294912 | tf_op jit(solution)/shard_map/all_gather | solution.py:123
  224.0 0.0 all-gather.3.cloned.1.call-update
  224.1 0.0 copy-done.6
  224.1 0.1 dynamic_slice.14
  224.2 0.0 copy-done.4
  224.2 58.3 %all-gather.3.cloned.1.call-done = bf16[256,8192]{1,0:T(8,128)(2,1)} async-done(((bf16[256,512]{1,0:T(8,128)(2,1)}), bf16[256,8192]{1,0:T(8,128)(2,1)}) %all-gather.3.cloned.1.call-update) | async-done | bytes 4194320 | tf_op jit(solution)/shard_map/all_gather | solution.py:125
  282.5 7.0 %fusion.35 = f32[256,512]{1,0:T(8,128)S(1)} fusion(bf16[256,8192]{1,0:T(8,128)(2,1)} %all-gather.3.cloned.1.call-done, bf16[8192,512]{1,0:T(8,128)(2,1)} %param.21), kind=kOutput, calls=%fused_computation.66 | convolution fusion | flops 2147483648 | bytes 13107200 | tf_op jit(solution)/shard_map/dot_general | solution.py:124
  289.5 0.3 collective-permute-start
  289.8 4.7 convert_reduce_fusion
  294.4 11.4 %collective-permute-done = f32[128,512]{1,0:T(8,128)S(1)} collective-permute-done((f32[128,512]{1,0:T(8,128)S(1)}, f32[128,512]{1,0:T(8,128)S(1)}, u32[]{:S(2)}, u32[]{:S(2)}) %collective-permute-start) | collective-permute-done | bytes 262176 | tf_op jit(solution)/shard_map/ppermute | solution.py:16
  305.8 0.2 exponential_reduce_fusion
  306.0 334.1 %psum.15 = f32[128]{0:T(128)S(1)} all-reduce(f32[128]{0:T(128)S(1)} %get-tuple-element.5), channel_id=1, replica_groups=mesh['stream'=2,'dp'=16,'tensor'=8] {'dp','tensor'}, use_global_device_ids=true, to_apply=%region_7.8 | all-reduce | flops 128 | bytes 1024 | tf_op jit(solution)/shard_map/psum | solution.py:143
  640.1 0.8 broadcast_subtract_fusion
  (17 shorter events, 0.2 us)
Async XLA Ops:
  6.5 14.6 %copy-start = (bf16[512,1024]{1,0:T(8,128)(2,1)S(1)}, bf16[512,1024]{1,0:T(8,128)(2,1)}, u32[]{:S(2)}) copy-start(bf16[512,1024]{1,0:T(8,128)(2,1)} %param.17) | copy-start | bytes 3145732
  6.5 160.0 %copy-start.3 = (bf16[1,32,512]{2,1,0:T(8,128)(2,1)S(1)}, bf16[1,32,512]{2,1,0:T(8,128)(2,1)}, u32[]{:S(2)}) copy-start(bf16[1,32,512]{2,1,0:T(8,128)(2,1)} %param.11) | copy-start | bytes 98308
  6.5 102.2 %copy-start.1 = (bf16[1,16,1,256,128]{4,3,2,1,0:T(8,128)(2,1)S(1)}, bf16[1,16,1,256,128]{4,3,2,1,0:T(8,128)(2,1)}, u32[]{:S(2)}) copy-start(bf16[1,16,1,256,128]{4,3,2,1,0:T(8,128)(2,1)} %param.13) | copy-start | bytes 3145732
  6.5 125.8 %copy-start.2 = (bf16[1024,512]{1,0:T(8,128)(2,1)S(1)}, bf16[1024,512]{1,0:T(8,128)(2,1)}, u32[]{:S(2)}) copy-start(bf16[1024,512]{1,0:T(8,128)(2,1)} %param.19) | copy-start | bytes 3145732
  6.5 127.1 %copy-start.5 = (bf16[512]{0:T(512)(128)(2,1)S(1)}, bf16[512]{0:T(512)(128)(2,1)}, u32[]{:S(2)}) copy-start(bf16[512]{0:T(512)(128)(2,1)} %param.20) | copy-start | bytes 3076
  6.5 217.5 %copy-start.6 = (f32[256]{0:T(256)S(1)}, f32[256]{0:T(256)}, u32[]{:S(2)}) copy-start(f32[256]{0:T(256)} %param.16) | copy-start | bytes 3076
  6.6 217.6 %copy-start.4 = (s32[256,128]{1,0:T(8,128)S(1)}, s32[256,128]{1,0:T(8,128)}, u32[]{:S(2)}) copy-start(s32[256,128]{1,0:T(8,128)} %param.15) | copy-start | bytes 393220
  6.6 98.2 %reduce-scatter.3.cloned.1.call-start = ((), (), s32[]{:S(2)}) async-start(), calls=%async_computation.2 | async-start | bytes 1392640 | tf_op jit(solution)/shard_map/reduce_scatter | solution.py:62
  24.0 142.5 %reduce-scatter.5.cloned.1.call-start = ((), (), s32[]{:S(2)}) async-start(), calls=%async_computation.3 | async-start | bytes 589824 | tf_op jit(solution)/shard_map/reduce_scatter | solution.py:117
  133.6 148.9 %all-gather.3.cloned.1.call-start = ((), (), s32[]{:S(2)}) async-start(), calls=%async_computation.4 | async-start | bytes 4456448 | tf_op jit(solution)/shard_map/all_gather | solution.py:125
  289.5 16.3 %collective-permute-start = (f32[128,512]{1,0:T(8,128)S(1)}, f32[128,512]{1,0:T(8,128)S(1)}, u32[]{:S(2)}, u32[]{:S(2)}) collective-permute-start(f32[128,512]{1,0:T(8,128)S(1)} %constant_dynamic-slice_fusion.1), channel_id=1, source_target_pairs={{0,128},{128,0},{1,129},{129,1},{2,130},{130,2},{3,131},{131,3},{4... | collective-permute-start | bytes 786440 | tf_op jit(solution)/shard_map/ppermute | solution.py:16
Sparse Core Ops, SparseCore 0:
  24.1 80.6 reduce-scatter.2
  133.7 32.7 reduce-scatter.4
  224.2 58.2 all-gather.2
where the time goes:
time: 648 us; the launch traced here: 647 us
  blocking collectives  427 us (66%)
  waiting for transfers between devices  182 us (28%)
  between operations  13.3 us (2%)
  matrix products  12.1 us (2%)
  other arithmetic  10.5 us (2%)
    psum x1, blocking collectives, body(): totals = lax.psum(jnp.sum(jnp.exp(guided), 1), ('dp', 'tensor'))  334 us
    reduce_scatter x1, waiting for transfers between devices, body(): lax.psum_scatter(jnp.concatenate([jnp.dot(all_rows, w_query, preferred_el...  79.2 us
    all_gather x1, waiting for transfers between devices, body(): lax.all_gather(normed_all, 'dp', axis=1, tiled=True)  58.3 us
    psum x1, blocking collectives, body(): squares = lax.psum(jnp.sum(widened * widened, 1), 'dp')  40.3 us
    reduce_scatter x1, waiting for transfers between devices, body(): lax.psum_scatter(partial_out, 'tensor', scatter_dimension=0, tiled=True)  32.9 us
    all_gather x1, blocking collectives, body(): lax.all_gather(attended, 'dp', axis=0, tiled=True)  23.3 us
    all_gather x1, blocking collectives, body(): normed_all = lax.all_gather(normed, 'tensor', axis=0, tiled=True)  15.3 us
    all_gather x1, blocking collectives, body(): all_rows = lax.all_gather(hidden[0], 'tensor', axis=0, tiled=True)  14.5 us
  transfers between devices with their start and end apart: 4, of which 4 were waited for; matrix products, arithmetic and copies ran while one was open for 1% of the time, Pallas kernels for 0%

commit v1 on v0

--- a/solution.py
+++ b/solution.py
@@ -140,7 +140,7 @@
     recent_mine = lax.dynamic_slice_in_dim(recent_ids, mine_start, half_rows, 0)
     guided = unconditional + guide * (conditional - unconditional)
     guided = guided - penalty_step * repeat_counts(recent_mine, column_base, vocab_local)
-    totals = lax.psum(jnp.sum(jnp.exp(guided), 1), ("dp", "tensor"))
+    totals = jnp.sum(lax.all_gather(jnp.sum(jnp.exp(guided), 1), ("dp", "tensor")), axis=0)
     return guided - jnp.log(totals)[:, None]
 
 

time: 648 us -> 501 us (0.77)
  blocking collectives: 427 us -> 275 us
    psum x1 -> x0, blocking collectives: 334 us -> none  [body(): totals = lax.psum(jnp.sum(jnp.exp(guided), 1), ('dp', 'tensor'))]
    all_gather x0 -> x1, blocking collectives: none -> 182 us  [body(): lax.all_gather(jnp.sum(jnp.exp(guided), 1), ('dp', 'tensor'))]
where the time goes in v1:
time: 501 us; the launch traced here: 495 us
  blocking collectives  275 us (55%)
  waiting for transfers between devices  182 us (36%)
  between operations  13.3 us (3%)
  matrix products  12.1 us (2%)
  other arithmetic  10.7 us (2%)
    all_gather x1, blocking collectives, body(): lax.all_gather(jnp.sum(jnp.exp(guided), 1), ('dp', 'tensor'))  182 us
    reduce_scatter x1, waiting for transfers between devices, body(): lax.psum_scatter(jnp.concatenate([jnp.dot(all_rows, w_query, preferred_el...  79.2 us
    all_gather x1, waiting for transfers between devices, body(): lax.all_gather(normed_all, 'dp', axis=1, tiled=True)  58.3 us
    psum x1, blocking collectives, body(): squares = lax.psum(jnp.sum(widened * widened, 1), 'dp')  40.3 us
    reduce_scatter x1, waiting for transfers between devices, body(): lax.psum_scatter(partial_out, 'tensor', scatter_dimension=0, tiled=True)  32.9 us
    all_gather x1, blocking collectives, body(): lax.all_gather(attended, 'dp', axis=0, tiled=True)  23.3 us
    all_gather x1, blocking collectives, body(): normed_all = lax.all_gather(normed, 'tensor', axis=0, tiled=True)  15.3 us
    all_gather x1, blocking collectives, body(): all_rows = lax.all_gather(hidden[0], 'tensor', axis=0, tiled=True)  14.5 us
  transfers between devices with their start and end apart: 4, of which 4 were waited for; matrix products, arithmetic and copies ran while one was open for 1% of the time, Pallas kernels for 0%

profile of v1, /device:TPU:128, one launch (start us, length us, event | category | flops | bytes accessed | tf_op | source)
XLA Modules:
  0.0 495.2 jit_solution(4983644203194290432)
XLA Ops:
  6.5 0.0 copy-start
  6.5 0.0 copy-start.6
  6.6 0.0 copy-start.4
  6.6 0.0 reduce-scatter.3.cloned.1.call-start
  6.6 14.5 %all-gather = bf16[1,256,512]{2,1,0:T(8,128)(2,1)S(1)} all-gather(bf16[1,32,512]{2,1,0:T(8,128)(2,1)} %param.11), channel_id=2, replica_groups=mesh['stream'=2,'dp'=16,'tensor'=8] {'tensor'}, dimensions={1}, use_global_device_ids=true | all-gather | bytes 294912 | tf_op jit(solution)/shard_map/all_gather | solution.py:60
  21.1 0.0 copy-done
  21.1 0.5 fusion.9
  21.6 1.2 fusion.5
  22.8 1.2 pad_maximum_fusion
  24.0 0.0 reduce-scatter.3.cloned.1.call-update
  24.0 0.0 reduce-scatter.5.cloned.1.call-start
  24.1 0.7 bitcast_convert_fusion
  24.7 0.7 iota_compare_fusion
  25.4 0.1 multiply_cosine_fusion.1
  25.6 79.2 %reduce-scatter.3.cloned.1.call-done = f32[16,1280]{1,0:T(8,128)} async-done(((f32[256,1280]{1,0:T(8,128)}), f32[16,1280]{1,0:T(8,128)}) %reduce-scatter.3.cloned.1.call-update) | async-done | bytes 81936 | tf_op jit(solution)/shard_map/reduce_scatter | solution.py:62
  104.8 0.7 slice.36
  105.6 0.1 fusion.30
  105.7 0.8 slice_bitcast_fusion
  106.6 0.1 maximum_bitcast_fusion
  106.6 0.1 subtract_convert_fusion
  106.7 0.2 fusion.25
  106.9 1.7 fusion.33
  108.7 0.0 copy-done.1
  108.7 0.3 fusion.2
  109.0 23.3 %all_gather.19 = bf16[256,1024]{1,0:T(8,128)(2,1)S(1)} all-gather(bf16[16,1024]{1,0:T(8,128)(2,1)S(1)} %bitcast.52), channel_id=1, replica_groups=mesh['stream'=2,'dp'=16,'tensor'=8] {'dp'}, dimensions={0}, use_global_device_ids=true | all-gather | bytes 557056 | tf_op jit(solution)/shard_map/all_gather | solution.py:113
  132.3 0.0 copy-done.2
  132.3 1.2 fusion.34
  133.5 0.0 reduce-scatter.5.cloned.1.call-update
  133.6 0.0 all-gather.5.cloned.1.call-start
  133.6 0.0 copy-done.5
  133.6 32.9 %reduce-scatter.5.cloned.1.call-done = f32[32,512]{1,0:T(8,128)} async-done(((f32[256,512]{1,0:T(8,128)}), f32[32,512]{1,0:T(8,128)}) %reduce-scatter.5.cloned.1.call-update) | async-done | bytes 65552 | tf_op jit(solution)/shard_map/reduce_scatter | solution.py:117
  166.5 0.0 copy-done.3
  166.5 1.0 fusion.11
  167.5 40.3 %psum.7 = f32[32]{0:T(128)S(1)} all-reduce(f32[32]{0:T(128)S(1)} %fusion.11), channel_id=1, replica_groups=mesh['stream'=2,'dp'=16,'tensor'=8] {'dp'}, use_global_device_ids=true, to_apply=%region_4.5 | all-reduce | flops 32 | bytes 256 | tf_op jit(solution)/shard_map/psum | solution.py:120
  207.8 0.9 fusion.13
  208.7 15.3 %all_gather.20 = bf16[256,512]{1,0:T(8,128)(2,1)} all-gather(bf16[32,512]{1,0:T(8,128)(2,1)S(1)} %fusion.13), channel_id=1, replica_groups=mesh['stream'=2,'dp'=16,'tensor'=8] {'tensor'}, dimensions={0}, use_global_device_ids=true | all-gather | bytes 294912 | tf_op jit(solution)/shard_map/all_gather | solution.py:123
  224.0 0.0 all-gather.5.cloned.1.call-update
  224.1 0.0 copy-done.6
  224.1 0.1 dynamic_slice.14
  224.2 58.3 %all-gather.5.cloned.1.call-done = bf16[256,8192]{1,0:T(8,128)(2,1)} async-done(((bf16[256,512]{1,0:T(8,128)(2,1)}), bf16[256,8192]{1,0:T(8,128)(2,1)}) %all-gather.5.cloned.1.call-update) | async-done | bytes 4194320 | tf_op jit(solution)/shard_map/all_gather | solution.py:125
  282.5 7.0 %fusion.35 = f32[256,512]{1,0:T(8,128)S(1)} fusion(bf16[256,8192]{1,0:T(8,128)(2,1)} %all-gather.5.cloned.1.call-done, bf16[8192,512]{1,0:T(8,128)(2,1)} %param.21), kind=kOutput, calls=%fused_computation.66 | convolution fusion | flops 2147483648 | bytes 13107200 | tf_op jit(solution)/shard_map/dot_general | solution.py:124
  289.5 0.3 collective-permute-start
  289.8 4.7 convert_reduce_fusion
  294.4 11.4 %collective-permute-done = f32[128,512]{1,0:T(8,128)S(1)} collective-permute-done((f32[128,512]{1,0:T(8,128)S(1)}, f32[128,512]{1,0:T(8,128)S(1)}, u32[]{:S(2)}, u32[]{:S(2)}) %collective-permute-start) | collective-permute-done | bytes 262176 | tf_op jit(solution)/shard_map/ppermute | solution.py:16
  305.8 0.2 exponential_reduce_fusion
  306.0 181.7 %all-gather.2 = f32[128,1,128]{2,1,0:T(1,128)S(1)} all-gather(f32[1,1,128]{2,1,0:T(1,128)S(1)} %bitcast.56), channel_id=3, replica_groups=mesh['stream'=2,'dp'=16,'tensor'=8] {'dp','tensor'}, dimensions={0}, use_global_device_ids=true | all-gather | bytes 66048 | tf_op jit(solution)/shard_map/all_gather | solution.py:143
  487.7 0.2 reduce_sum.49
  487.9 0.8 broadcast_subtract_fusion
  (18 shorter events, 0.2 us)
Async XLA Ops:
  6.5 14.6 %copy-start = (bf16[512,1024]{1,0:T(8,128)(2,1)S(1)}, bf16[512,1024]{1,0:T(8,128)(2,1)}, u32[]{:S(2)}) copy-start(bf16[512,1024]{1,0:T(8,128)(2,1)} %param.17) | copy-start | bytes 3145732
  6.5 160.0 %copy-start.3 = (bf16[1,32,512]{2,1,0:T(8,128)(2,1)S(1)}, bf16[1,32,512]{2,1,0:T(8,128)(2,1)}, u32[]{:S(2)}) copy-start(bf16[1,32,512]{2,1,0:T(8,128)(2,1)} %param.11) | copy-start | bytes 98308
  6.5 102.2 %copy-start.1 = (bf16[1,16,1,256,128]{4,3,2,1,0:T(8,128)(2,1)S(1)}, bf16[1,16,1,256,128]{4,3,2,1,0:T(8,128)(2,1)}, u32[]{:S(2)}) copy-start(bf16[1,16,1,256,128]{4,3,2,1,0:T(8,128)(2,1)} %param.13) | copy-start | bytes 3145732
  6.5 125.8 %copy-start.2 = (bf16[1024,512]{1,0:T(8,128)(2,1)S(1)}, bf16[1024,512]{1,0:T(8,128)(2,1)}, u32[]{:S(2)}) copy-start(bf16[1024,512]{1,0:T(8,128)(2,1)} %param.19) | copy-start | bytes 3145732
  6.5 127.1 %copy-start.5 = (bf16[512]{0:T(512)(128)(2,1)S(1)}, bf16[512]{0:T(512)(128)(2,1)}, u32[]{:S(2)}) copy-start(bf16[512]{0:T(512)(128)(2,1)} %param.20) | copy-start | bytes 3076
  6.5 217.5 %copy-start.6 = (f32[256]{0:T(256)S(1)}, f32[256]{0:T(256)}, u32[]{:S(2)}) copy-start(f32[256]{0:T(256)} %param.16) | copy-start | bytes 3076
  6.6 217.6 %copy-start.4 = (s32[256,128]{1,0:T(8,128)S(1)}, s32[256,128]{1,0:T(8,128)}, u32[]{:S(2)}) copy-start(s32[256,128]{1,0:T(8,128)} %param.15) | copy-start | bytes 393220
  6.6 98.2 %reduce-scatter.3.cloned.1.call-start = ((), (), s32[]{:S(2)}) async-start(), calls=%async_computation.2 | async-start | bytes 1392640 | tf_op jit(solution)/shard_map/reduce_scatter | solution.py:62
  24.0 142.5 %reduce-scatter.5.cloned.1.call-start = ((), (), s32[]{:S(2)}) async-start(), calls=%async_computation.3 | async-start | bytes 589824 | tf_op jit(solution)/shard_map/reduce_scatter | solution.py:117
  133.6 148.9 %all-gather.5.cloned.1.call-start = ((), (), s32[]{:S(2)}) async-start(), calls=%async_computation.4 | async-start | bytes 4456448 | tf_op jit(solution)/shard_map/all_gather | solution.py:125
  289.5 16.3 %collective-permute-start = (f32[128,512]{1,0:T(8,128)S(1)}, f32[128,512]{1,0:T(8,128)S(1)}, u32[]{:S(2)}, u32[]{:S(2)}) collective-permute-start(f32[128,512]{1,0:T(8,128)S(1)} %constant_dynamic-slice_fusion.1), channel_id=1, source_target_pairs={{0,128},{128,0},{1,129},{129,1},{2,130},{130,2},{3,131},{131,3},{4... | collective-permute-start | bytes 786440 | tf_op jit(solution)/shard_map/ppermute | solution.py:16
Sparse Core Ops, SparseCore 0:
  24.1 80.6 reduce-scatter.2
  133.7 32.7 reduce-scatter.4
  224.2 58.2 all-gather.4
